TPU v7x, 512 devices: a whole 4x8x8 slice. The times are simulated.
512 devices in a mesh: row: 32 (over y, x), col: 16 (over z, core).
Axes of the slice: x: 4, y: 8, z: 8, core: 2. Of those that a mesh axis runs over, the one named last changes fastest.
Arguments:
- right_side: float32 [64, 16384], P(None, ('row', 'col')), may hold values from -6 to 6
- regular: float32 [16384], P(('row', 'col')), may hold values from 1 to 2
- curvature: bfloat16 [32, 32, 16, 128, 128], P('row', None, 'col'), as said below
- block_rows: int32 [32, 32, 16], P('row', None, 'col'), may hold values from 0 to 3, as said below
- block_cols: int32 [32, 32, 16], P('row', None, 'col'), may hold values from 0 to 3
- block_counts: int32 [32, 32, 16], P('row', None, 'col'), may hold values from 0 to 1, as said below
Outputs:
- solution: float32 [64, 16384], P(None, ('row', 'col'))
- residual: float32 [64, 16384], P(None, ('row', 'col'))
Inputs may be any that keep to these rules, and one draw needn't show every extreme that they name: `block_rows`: the curvature is symmetric: a live term of owner r from source s with block row a and block column b is matched, in the same slot of owner s from source r, by block row b, block column a and the transposed block. `block_counts`: counts for the first index of col are always 1. A with this curvature and regular is symmetric positive definite.
All inputs are finite; a program needn't handle non-finite values.
Results may differ from a plain program's by a relative error of at most 0.0041.
Values may be sent and summed in bfloat16 or wider, within the bound.
No kernel may reach another device: no remote copies, remote signals or barrier semaphores. Data moves between devices by JAX's collectives and lax.ppermute only.
A program may use at most 64 MiB of HBM per device.

v0:
```python
import jax
import jax.numpy as jnp
from jax import lax
from jax.sharding import Mesh
from jax.sharding import PartitionSpec as P

M_DEV = 1
ITERS = 3
COL = ("col_0", "col_1")
ROW_COL = ("row_0", "row_1", "col_0", "col_1")
ROW = ("row_0", "row_1")


def one_axis_at_a_time(shard, axes):
    for axis in axes:
        shard = lax.psum(shard, axis)
    return shard


def gather_axes(shard, axes, dim):
    for axis in reversed(axes):
        shard = lax.all_gather(shard, axis, axis=dim, tiled=True)
    return shard


def in_blocks(shard, dim, peers):
    shape = shard.shape
    blocks = shard.reshape(*shape[:dim], peers, shape[dim] // peers, *shape[dim + 1 :])
    return jnp.moveaxis(blocks, dim, 0)


def sum_at_owner(shard, axis, dim):
    peers = lax.axis_size(axis)
    blocks = lax.all_to_all(in_blocks(shard, dim, peers), axis, 0, 0, tiled=True)
    return jnp.sum(blocks, axis=0)


def chol_solve(matrix, rhs_mat):
    factor = jnp.linalg.cholesky(matrix)
    return jax.scipy.linalg.cho_solve((factor, True), rhs_mat)


def local_gram(left, right):
    return jnp.dot(left, right.T, precision=lax.Precision.HIGHEST)


def live_table(counts_local):
    per_slot = jnp.repeat(counts_local, M_DEV, axis=1)
    slot_rank = jnp.arange(per_slot.shape[1], dtype=jnp.int32) % M_DEV
    return slot_rank[None, :] < per_slot


def apply_terms(dir_piece, curv_local, rows_local, cols_local, live_local, blocks_dev):
    samples = dir_piece.shape[0]
    sources = dir_piece.shape[1]
    block_len = curv_local.shape[-1]
    slot_cap = curv_local.shape[1]
    flat_dirs = dir_piece.reshape(samples, sources * blocks_dev, block_len)
    positions = (jnp.arange(sources, dtype=jnp.int32)[:, None] * blocks_dev + cols_local).reshape(
        -1
    )
    chosen = jnp.take(flat_dirs, positions, axis=1).reshape(samples, sources, slot_cap, block_len)
    products = jnp.einsum("xsmq,smpq->xsmp", chosen, curv_local, preferred_element_type=jnp.float32)
    block_ids = jnp.arange(blocks_dev, dtype=jnp.int32)
    row_table = (
        (rows_local[:, :, None] == block_ids[None, None, :]) & live_local[:, :, None]
    ).astype(jnp.float32)
    return jnp.einsum("xsmp,smb->xbp", products, row_table, precision=lax.Precision.HIGHEST)


def body(right_side, regular, curvature, block_rows, block_cols, block_counts):
    samples = right_side.shape[0]
    pix_here = right_side.shape[1]
    block_len = curvature.shape[-1]
    blocks_dev = pix_here * lax.axis_size(COL) // block_len
    curv_local = curvature[0]
    rows_local = block_rows[0]
    cols_local = block_cols[0]
    live_local = live_table(block_counts[0])
    solution = jnp.zeros_like(right_side)
    residual = right_side
    direction = right_side
    res_gram = one_axis_at_a_time(local_gram(residual, residual), ROW_COL)
    for iteration in range(ITERS):
        dir_bf = direction.astype(jnp.bfloat16)
        own_rows = lax.all_gather(dir_bf, COL, axis=1, tiled=True)
        partials = apply_terms(
            gather_axes(own_rows[:, None, :], ROW, 1),
            curv_local,
            rows_local,
            cols_local,
            live_local,
            blocks_dev,
        )
        coupled = sum_at_owner(partials.reshape(samples, blocks_dev * block_len), COL, 1)
        image = regular[None, :] * direction + coupled
        curv_gram, cross_gram, image_gram = (
            one_axis_at_a_time(local_gram(direction, image), ROW_COL),
            one_axis_at_a_time(local_gram(residual, image), ROW_COL),
            one_axis_at_a_time(local_gram(image, image), ROW_COL),
        )
        curv_gram = 0.5 * (curv_gram + curv_gram.T)
        alpha_mat = chol_solve(curv_gram, res_gram)
        solution = solution + jnp.dot(alpha_mat.T, direction, precision=lax.Precision.HIGHEST)
        residual = residual - jnp.dot(alpha_mat.T, image, precision=lax.Precision.HIGHEST)
        cross_term = jnp.dot(cross_gram, alpha_mat, precision=lax.Precision.HIGHEST)
        quad_term = jnp.dot(
            alpha_mat.T,
            jnp.dot(image_gram, alpha_mat, precision=lax.Precision.HIGHEST),
            precision=lax.Precision.HIGHEST,
        )
        new_gram = res_gram - cross_term - cross_term.T + quad_term
        new_gram = 0.5 * (new_gram + new_gram.T)
        if iteration + 1 < ITERS:
            beta_mat = chol_solve(res_gram, new_gram)
            direction = residual + jnp.dot(beta_mat.T, direction, precision=lax.Precision.HIGHEST)
            res_gram = new_gram
    return (solution, residual)


def solution(mesh):
    finer = Mesh(mesh.devices.reshape(8, 4, 8, 2), ("row_0", "row_1", "col_0", "col_1"))
    placed = (
        P(None, ROW_COL),
        P(ROW_COL),
        P(ROW, None, COL, None, None),
        P(ROW, None, COL),
        P(ROW, None, COL),
        P(ROW, None, COL),
    )
    return jax.shard_map(
        body,
        mesh=finer,
        in_specs=placed,
        out_specs=(P(None, ROW_COL), P(None, ROW_COL)),
        check_vma=False,
    )
```

profile of v0, /device:TPU:1, one launch (start us, length us, event | category | flops | bytes accessed | tf_op | source)
XLA Modules:
  0.0 618.6 jit_solution(11180150527277156011)
XLA Ops:
  8.0 24.8 %all_gather.27 = bf16[64,512]{0,1:T(8,128)(2,1)S(1)} all-gather(bf16[64,32]{0,1:T(8,128)(2,1)S(1)} %convert_element_type.12), channel_id=1, replica_groups=mesh['row_0'=8,'row_1'=4,'col_0'=8,'col_1'=2] {'col_0','col_1'}, dimensions={1}, use_global_device_ids=true | all-gather | bytes 69632 | tf_op jit(solution)/shard_map/all_gather | solution.py:86
  32.8 11.0 %all-gather = bf16[64,2048]{0,1:T(8,128)(2,1)S(1)} all-gather(bf16[64,512]{0,1:T(8,128)(2,1)S(1)} %all_gather.27), channel_id=2, replica_groups=mesh['row_0'=8,'row_1'=4,'col_0'=8,'col_1'=2] {'row_1'}, dimensions={1}, use_global_device_ids=true | all-gather | bytes 327680 | tf_op jit(solution)/shard_map/all_gather | solution.py:22
  46.1 36.7 %all-gather.7.cloned.1.call-done = bf16[64,32,512]{2,0,1:T(8,128)(2,1)} async-done(((bf16[64,4,512]{2,0,1:T(8,128)(2,1)}), bf16[64,32,512]{2,0,1:T(8,128)(2,1)}) %all-gather.7.cloned.1.call-update) | async-done | bytes 2097168 | tf_op jit(solution)/shard_map/all_gather | solution.py:22
  96.5 12.2 %all-to-all-start = ((f32[16,1,2048]{2,1,0:T(1,128)}), f32[16,1,2048]{2,1,0:T(1,128)S(1)}, u32[]{:S(2)}, u32[]{:S(2)}) async-start(f32[16,1,2048]{2,1,0:T(1,128)} %reshape.231), calls=%async_computation | async-start | bytes 262144 | tf_op jit(solution)/shard_map/all_to_all | solution.py:34
  119.8 22.9 %all-reduce.3 = (f32[64,64]{0,1:T(8,128)S(1)}, f32[64,64]{1,0:T(8,128)S(1)}, f32[64,64]{1,0:T(8,128)S(1)}) all-reduce(f32[64,64]{0,1:T(8,128)S(1)} %fusion.74, f32[64,64]{1,0:T(8,128)S(1)} %convolution_bitcast_fusion.6, f32[64,64]{1,0:T(8,128)S(1)} %fusion.54), channel_id=1, replica_groups=mesh['row_0'=8,'row_1'=4,'col_0'=8,'col_1'=2] {'row_0'}, use_global_device_ids=true, to_apply=%region_7.10 | all-reduce | flops 12288 | bytes 98304 | tf_op jit(solution)/shard_map/psum | solution.py:16
  142.7 14.2 %all-reduce.5 = (f32[64,64]{0,1:T(8,128)S(1)}, f32[64,64]{1,0:T(8,128)S(1)}, f32[64,64]{1,0:T(8,128)S(1)}) all-reduce(f32[64,64]{0,1:T(8,128)S(1)} %get-tuple-element.14, f32[64,64]{1,0:T(8,128)S(1)} %get-tuple-element.15, f32[64,64]{1,0:T(8,128)S(1)} %get-tuple-element.16), channel_id=1, replica_groups=mesh['row_0'=8,'row_1'=4,'col_0'=8,'col_1'=2] {'row_1'}, use_global_device_ids=true, to_apply=%region_8.11 | all-reduce | flops 12288 | bytes 98304 | tf_op jit(solution)/shard_map/psum | solution.py:16
  156.9 21.7 %all-reduce.1 = (f32[64,64]{0,1:T(8,128)S(1)}, f32[64,64]{1,0:T(8,128)S(1)}, f32[64,64]{1,0:T(8,128)S(1)}) all-reduce(f32[64,64]{0,1:T(8,128)S(1)} %get-tuple-element.20, f32[64,64]{1,0:T(8,128)S(1)} %get-tuple-element.21, f32[64,64]{1,0:T(8,128)S(1)} %get-tuple-element.22), channel_id=1, replica_groups=mesh['row_0'=8,'row_1'=4,'col_0'=8,'col_1'=2] {'col_0'}, use_global_device_ids=true, to_apply=%region_9.12 | all-reduce | flops 12288 | bytes 98304 | tf_op jit(solution)/shard_map/psum | solution.py:16
  178.6 21.3 %all-reduce.7 = (f32[64,64]{0,1:T(8,128)S(1)}, f32[64,64]{1,0:T(8,128)S(1)}, f32[64,64]{1,0:T(8,128)S(1)}) all-reduce(f32[64,64]{0,1:T(8,128)S(1)} %get-tuple-element.8, f32[64,64]{1,0:T(8,128)S(1)} %get-tuple-element.9, f32[64,64]{1,0:T(8,128)S(1)} %get-tuple-element.10), channel_id=1, replica_groups=mesh['row_0'=8,'row_1'=4,'col_0'=8,'col_1'=2] {'col_1'}, use_global_device_ids=true, to_apply=%region_10.13 | all-reduce | flops 12288 | bytes 98304 | tf_op jit(solution)/shard_map/psum | solution.py:16
  226.3 15.8 %all_gather.30 = bf16[64,512]{0,1:T(8,128)(2,1)S(1)} all-gather(bf16[64,32]{0,1:T(8,128)(2,1)S(1)} %get-tuple-element.31), channel_id=1, replica_groups=mesh['row_0'=8,'row_1'=4,'col_0'=8,'col_1'=2] {'col_0','col_1'}, dimensions={1}, use_global_device_ids=true | all-gather | bytes 69632 | tf_op jit(solution)/shard_map/all_gather | solution.py:86
  242.2 10.3 %all-gather.1 = bf16[64,2048]{0,1:T(8,128)(2,1)S(1)} all-gather(bf16[64,512]{0,1:T(8,128)(2,1)S(1)} %all_gather.30), channel_id=3, replica_groups=mesh['row_0'=8,'row_1'=4,'col_0'=8,'col_1'=2] {'row_1'}, dimensions={1}, use_global_device_ids=true | all-gather | bytes 327680 | tf_op jit(solution)/shard_map/all_gather | solution.py:22
  259.4 30.4 %all-gather.9.cloned.1.call-done = bf16[64,32,512]{2,0,1:T(8,128)(2,1)} async-done(((bf16[64,4,512]{2,0,1:T(8,128)(2,1)}), bf16[64,32,512]{2,0,1:T(8,128)(2,1)}) %all-gather.9.cloned.1.call-update) | async-done | bytes 2097168 | tf_op jit(solution)/shard_map/all_gather | solution.py:22
  303.5 12.2 %all-to-all-start.1 = ((f32[16,1,2048]{2,1,0:T(1,128)}), f32[16,1,2048]{2,1,0:T(1,128)S(1)}, u32[]{:S(2)}, u32[]{:S(2)}) async-start(f32[16,1,2048]{2,1,0:T(1,128)} %reshape.233), calls=%async_computation.1 | async-start | bytes 262144 | tf_op jit(solution)/shard_map/all_to_all | solution.py:34
  326.5 22.9 %all-reduce.2 = (f32[64,64]{1,0:T(8,128)S(1)}, f32[64,64]{1,0:T(8,128)S(1)}, f32[64,64]{1,0:T(8,128)S(1)}) all-reduce(f32[64,64]{1,0:T(8,128)S(1)} %fusion.78, f32[64,64]{1,0:T(8,128)S(1)} %fusion.81, f32[64,64]{1,0:T(8,128)S(1)} %fusion.79), channel_id=1, replica_groups=mesh['row_0'=8,'row_1'=4,'col_0'=8,'col_1'=2] {'row_0'}, use_global_device_ids=true, to_apply=%region_16.20 | all-reduce | flops 12288 | bytes 98304 | tf_op jit(solution)/shard_map/psum | solution.py:16
  349.4 14.2 %all-reduce.4 = (f32[64,64]{1,0:T(8,128)S(1)}, f32[64,64]{1,0:T(8,128)S(1)}, f32[64,64]{1,0:T(8,128)S(1)}) all-reduce(f32[64,64]{1,0:T(8,128)S(1)} %get-tuple-element.11, f32[64,64]{1,0:T(8,128)S(1)} %get-tuple-element.12, f32[64,64]{1,0:T(8,128)S(1)} %get-tuple-element.13), channel_id=1, replica_groups=mesh['row_0'=8,'row_1'=4,'col_0'=8,'col_1'=2] {'row_1'}, use_global_device_ids=true, to_apply=%region_17.21 | all-reduce | flops 12288 | bytes 98304 | tf_op jit(solution)/shard_map/psum | solution.py:16
  363.6 21.6 %all-reduce = (f32[64,64]{1,0:T(8,128)S(1)}, f32[64,64]{1,0:T(8,128)S(1)}, f32[64,64]{1,0:T(8,128)S(1)}) all-reduce(f32[64,64]{1,0:T(8,128)S(1)} %get-tuple-element.17, f32[64,64]{1,0:T(8,128)S(1)} %get-tuple-element.18, f32[64,64]{1,0:T(8,128)S(1)} %get-tuple-element.19), channel_id=1, replica_groups=mesh['row_0'=8,'row_1'=4,'col_0'=8,'col_1'=2] {'col_0'}, use_global_device_ids=true, to_apply=%region_18.22 | all-reduce | flops 12288 | bytes 98304 | tf_op jit(solution)/shard_map/psum | solution.py:16
  385.2 21.5 %all-reduce.6 = (f32[64,64]{1,0:T(8,128)S(1)}, f32[64,64]{1,0:T(8,128)S(1)}, f32[64,64]{1,0:T(8,128)S(1)}) all-reduce(f32[64,64]{1,0:T(8,128)S(1)} %get-tuple-element.4, f32[64,64]{1,0:T(8,128)S(1)} %get-tuple-element.6, f32[64,64]{1,0:T(8,128)S(1)} %get-tuple-element.7), channel_id=1, replica_groups=mesh['row_0'=8,'row_1'=4,'col_0'=8,'col_1'=2] {'col_1'}, use_global_device_ids=true, to_apply=%region_19.23 | all-reduce | flops 12288 | bytes 98304 | tf_op jit(solution)/shard_map/psum | solution.py:16
  420.9 15.6 %all_gather.33 = bf16[64,512]{0,1:T(8,128)(2,1)S(1)} all-gather(bf16[64,32]{0,1:T(8,128)(2,1)S(1)} %get-tuple-element.33), channel_id=1, replica_groups=mesh['row_0'=8,'row_1'=4,'col_0'=8,'col_1'=2] {'col_0','col_1'}, dimensions={1}, use_global_device_ids=true | all-gather | bytes 69632 | tf_op jit(solution)/shard_map/all_gather | solution.py:86
  436.4 10.3 %all-gather.2 = bf16[64,2048]{0,1:T(8,128)(2,1)S(1)} all-gather(bf16[64,512]{0,1:T(8,128)(2,1)S(1)} %all_gather.33), channel_id=4, replica_groups=mesh['row_0'=8,'row_1'=4,'col_0'=8,'col_1'=2] {'row_1'}, dimensions={1}, use_global_device_ids=true | all-gather | bytes 327680 | tf_op jit(solution)/shard_map/all_gather | solution.py:22
  447.6 37.4 %all-gather.11.cloned.1.call-done = bf16[64,32,512]{2,0,1:T(8,128)(2,1)} async-done(((bf16[64,4,512]{2,0,1:T(8,128)(2,1)}), bf16[64,32,512]{2,0,1:T(8,128)(2,1)}) %all-gather.11.cloned.1.call-update) | async-done | bytes 2097168 | tf_op jit(solution)/shard_map/all_gather | solution.py:22
  498.7 12.2 %all-to-all-start.2 = ((f32[16,1,2048]{2,1,0:T(1,128)}), f32[16,1,2048]{2,1,0:T(1,128)S(1)}, u32[]{:S(2)}, u32[]{:S(2)}) async-start(f32[16,1,2048]{2,1,0:T(1,128)} %reshape.235), calls=%async_computation.2 | async-start | bytes 262144 | tf_op jit(solution)/shard_map/all_to_all | solution.py:34
  521.1 22.1 %psum.232 = f32[64,64]{1,0:T(8,128)S(1)} all-reduce(f32[64,64]{1,0:T(8,128)S(1)} %fusion.53), channel_id=1, replica_groups=mesh['row_0'=8,'row_1'=4,'col_0'=8,'col_1'=2] {'row_0'}, use_global_device_ids=true, to_apply=%region_29.33 | all-reduce | flops 4096 | bytes 32768 | tf_op jit(solution)/shard_map/psum | solution.py:16
  543.2 13.2 %psum.233 = f32[64,64]{1,0:T(8,128)S(1)} all-reduce(f32[64,64]{1,0:T(8,128)S(1)} %psum.232), channel_id=1, replica_groups=mesh['row_0'=8,'row_1'=4,'col_0'=8,'col_1'=2] {'row_1'}, use_global_device_ids=true, to_apply=%region_30.34 | all-reduce | flops 4096 | bytes 32768 | tf_op jit(solution)/shard_map/psum | solution.py:16
  556.4 20.4 %psum.234 = f32[64,64]{1,0:T(8,128)S(1)} all-reduce(f32[64,64]{1,0:T(8,128)S(1)} %psum.233), channel_id=1, replica_groups=mesh['row_0'=8,'row_1'=4,'col_0'=8,'col_1'=2] {'col_0'}, use_global_device_ids=true, to_apply=%region_31.35 | all-reduce | flops 4096 | bytes 32768 | tf_op jit(solution)/shard_map/psum | solution.py:16
  576.8 21.0 %psum.235 = f32[64,64]{1,0:T(8,128)S(1)} all-reduce(f32[64,64]{1,0:T(8,128)S(1)} %psum.234), channel_id=1, replica_groups=mesh['row_0'=8,'row_1'=4,'col_0'=8,'col_1'=2] {'col_1'}, use_global_device_ids=true, to_apply=%region_32.36 | all-reduce | flops 4096 | bytes 32768 | tf_op jit(solution)/shard_map/psum | solution.py:16
  (137 shorter events, 138.3 us)
Async XLA Ops:
  7.2 85.4 %copy-start = (bf16[1,32,1,128,128]{4,3,2,1,0:T(8,128)(2,1)S(1)}, bf16[1,32,1,128,128]{4,3,2,1,0:T(8,128)(2,1)}, u32[]{:S(2)}) copy-start(bf16[1,32,1,128,128]{4,3,2,1,0:T(8,128)(2,1)} %param.13) | copy-start | bytes 3145732
  7.2 75.7 %all-gather.7.cloned.1.call-start = ((), (), s32[]{:S(2)}) async-start(), calls=%async_computation.3 | async-start | bytes 2359296 | tf_op jit(solution)/shard_map/all_gather | solution.py:22
  91.2 3.3 copy-start.3
  92.6 16.2 %copy-start.1 = (f32[64,32]{0,1:T(8,128)S(1)}, f32[64,32]{0,1:T(8,128)}, u32[]{:S(2)}) copy-start(f32[64,32]{0,1:T(8,128)} %param.11) | copy-start | bytes 24580
  94.5 24.7 %copy-start.2 = (f32[32]{0:T(128)S(1)}, f32[32]{0:T(128)}, u32[]{:S(2)}) copy-start(f32[32]{0:T(128)} %param.12) | copy-start | bytes 388
  96.5 21.1 %all-to-all-start = ((f32[16,1,2048]{2,1,0:T(1,128)}), f32[16,1,2048]{2,1,0:T(1,128)S(1)}, u32[]{:S(2)}, u32[]{:S(2)}) async-start(f32[16,1,2048]{2,1,0:T(1,128)} %reshape.231), calls=%async_computation | async-start | bytes 262144 | tf_op jit(solution)/shard_map/all_to_all | solution.py:34
  108.7 181.2 %all-gather.9.cloned.1.call-start = ((), (), s32[]{:S(2)}) async-start(), calls=%async_computation.4 | async-start | bytes 2359296 | tf_op jit(solution)/shard_map/all_gather | solution.py:22
  303.5 21.1 %all-to-all-start.1 = ((f32[16,1,2048]{2,1,0:T(1,128)}), f32[16,1,2048]{2,1,0:T(1,128)S(1)}, u32[]{:S(2)}, u32[]{:S(2)}) async-start(f32[16,1,2048]{2,1,0:T(1,128)} %reshape.233), calls=%async_computation.1 | async-start | bytes 262144 | tf_op jit(solution)/shard_map/all_to_all | solution.py:34
  315.7 169.4 %all-gather.11.cloned.1.call-start = ((), (), s32[]{:S(2)}) async-start(), calls=%async_computation.5 | async-start | bytes 2359296 | tf_op jit(solution)/shard_map/all_gather | solution.py:22
  498.7 21.1 %all-to-all-start.2 = ((f32[16,1,2048]{2,1,0:T(1,128)}), f32[16,1,2048]{2,1,0:T(1,128)S(1)}, u32[]{:S(2)}, u32[]{:S(2)}) async-start(f32[16,1,2048]{2,1,0:T(1,128)} %reshape.235), calls=%async_computation.2 | async-start | bytes 262144 | tf_op jit(solution)/shard_map/all_to_all | solution.py:34
Sparse Core Ops, SparseCore 0:
  44.9 37.8 all-gather.6
  253.5 36.3 all-gather.8
  447.8 37.2 all-gather.10
where the time goes:
time: 620 us; the launch traced here: 619 us
  blocking collectives  325 us (52%)
  waiting for transfers between devices  124 us (20%)
  other arithmetic  65.6 us (11%)
  starting transfers between devices  37 us (6%)
  local copies, waits for them, and re-layouts  36.5 us (6%)
  matrix products  16.2 us (3%)
  between operations  14.4 us (2%)
    psum x12, blocking collectives, one_axis_at_a_time(): shard = lax.psum(shard, axis)  237 us
    all_gather x3, waiting for transfers between devices, gather_axes(): shard = lax.all_gather(shard, axis, axis=dim, tiled=True)  105 us
    all_gather x3, blocking collectives, body(): own_rows = lax.all_gather(dir_bf, COL, axis=1, tiled=True)  56.2 us
    all_to_all x3, starting transfers between devices, sum_at_owner(): lax.all_to_all(in_blocks(shard, dim, peers), axis, 0, 0, tiled=True)  36.7 us
    another operation x15, other arithmetic, chol_solve(): factor = jnp.linalg.cholesky(matrix)  32.6 us
    all_gather x3, blocking collectives, gather_axes(): shard = lax.all_gather(shard, axis, axis=dim, tiled=True)  31.5 us
    another operation x10, other arithmetic, chol_solve(): return jax.scipy.linalg.cho_solve((factor, True), rhs_mat)  27.7 us
    all_to_all x3, waiting for transfers between devices, sum_at_owner(): lax.all_to_all(in_blocks(shard, dim, peers), axis, 0, 0, tiled=True)  19.6 us
  transfers between devices with their start and end apart: 6, of which 6 were waited for; matrix products, arithmetic and copies ran while one was open for 2% of the time, Pallas kernels for 0%

commit v1 on v0

--- a/solution.py
+++ b/solution.py
@@ -1,3 +1,4 @@
+import functools
 import jax
 import jax.numpy as jnp
 from jax import lax
@@ -9,6 +10,19 @@
 COL = ("col_0", "col_1")
 ROW_COL = ("row_0", "row_1", "col_0", "col_1")
 ROW = ("row_0", "row_1")
+
+
+def sheet_note(values, axis_id):
+    long_array = jnp.concatenate(
+        jax.lax.all_to_all(
+            jnp.stack(tuple((values for _ in range(jax.lax.axis_size(axis_id))))), axis_id, 0, 0
+        ),
+        1,
+    )
+    return long_array
+
+
+skins_advance = functools.partial(sheet_note, axis_id=COL)
 
 
 def one_axis_at_a_time(shard, axes):
@@ -83,7 +97,7 @@
     res_gram = one_axis_at_a_time(local_gram(residual, residual), ROW_COL)
     for iteration in range(ITERS):
         dir_bf = direction.astype(jnp.bfloat16)
-        own_rows = lax.all_gather(dir_bf, COL, axis=1, tiled=True)
+        own_rows = skins_advance(dir_bf)
         partials = apply_terms(
             gather_axes(own_rows[:, None, :], ROW, 1),
             curv_local,

time: 620 us -> 601 us (0.969)
  blocking collectives: 325 us -> 312 us
    all_gather x3 -> x0, blocking collectives: 56.2 us -> none  [body(): own_rows = lax.all_gather(dir_bf, COL, axis=1, tiled=True)]
    all_to_all x0 -> x3, blocking collectives: none -> 44.2 us  [sheet_note(): jax.lax.all_to_all(jnp.stack(tuple((values for _ in range(jax.lax.axis_si...]
where the time goes in v1:
time: 601 us; the launch traced here: 600 us
  blocking collectives  312 us (52%)
  waiting for transfers between devices  120 us (20%)
  other arithmetic  65.6 us (11%)
  starting transfers between devices  36.9 us (6%)
  local copies, waits for them, and re-layouts  34.9 us (6%)
  matrix products  16.2 us (3%)
  between operations  14.5 us (2%)
    psum x12, blocking collectives, one_axis_at_a_time(): shard = lax.psum(shard, axis)  237 us
    all_gather x3, waiting for transfers between devices, gather_axes(): shard = lax.all_gather(shard, axis, axis=dim, tiled=True)  100 us
    all_to_all x3, blocking collectives, sheet_note(): jax.lax.all_to_all(jnp.stack(tuple((values for _ in range(jax.lax.axis_si...  44.2 us
    all_to_all x3, starting transfers between devices, sum_at_owner(): lax.all_to_all(in_blocks(shard, dim, peers), axis, 0, 0, tiled=True)  36.6 us
    another operation x15, other arithmetic, chol_solve(): factor = jnp.linalg.cholesky(matrix)  32.6 us
    all_gather x3, blocking collectives, gather_axes(): shard = lax.all_gather(shard, axis, axis=dim, tiled=True)  30.7 us
    another operation x10, other arithmetic, chol_solve(): return jax.scipy.linalg.cho_solve((factor, True), rhs_mat)  27.7 us
    all_to_all x3, waiting for transfers between devices, sum_at_owner(): lax.all_to_all(in_blocks(shard, dim, peers), axis, 0, 0, tiled=True)  19.6 us
  transfers between devices with their start and end apart: 6, of which 6 were waited for; matrix products, arithmetic and copies ran while one was open for 2% of the time, Pallas kernels for 0%

profile of v1, /device:TPU:1, one launch (start us, length us, event | category | flops | bytes accessed | tf_op | source)
XLA Modules:
  0.0 600.0 jit_solution(7826365500098160287)
XLA Ops:
  8.2 19.4 %all_to_all.30 = bf16[16,2,1024]{2,1,0:T(2,128)(2,1)S(1)} all-to-all(bf16[16,2,1024]{2,1,0:T(2,128)(2,1)S(1)} %reshape.246), channel_id=1, replica_groups=mesh['row_0'=8,'row_1'=4,'col_0'=8,'col_1'=2] {'col_0','col_1'}, dimensions={0} | all-to-all | bytes 131072 | tf_op jit(solution)/shard_map/all_to_all | solution.py:17
  27.8 10.5 %all_gather.18 = bf16[64,4,512]{2,0,1:T(8,128)(2,1)} all-gather(bf16[64,1,512]{2,0,1:T(8,128)(2,1)S(1)} %copy.83), channel_id=1, replica_groups=mesh['row_0'=8,'row_1'=4,'col_0'=8,'col_1'=2] {'row_1'}, dimensions={1}, use_global_device_ids=true | all-gather | bytes 327680 | tf_op jit(solution)/shard_map/all_gather | solution.py:36
  39.6 36.6 %all-gather.4.cloned.1.call-done = bf16[64,32,512]{2,0,1:T(8,128)(2,1)} async-done(((bf16[64,4,512]{2,0,1:T(8,128)(2,1)}), bf16[64,32,512]{2,0,1:T(8,128)(2,1)}) %all-gather.4.cloned.1.call-update) | async-done | bytes 2097168 | tf_op jit(solution)/shard_map/all_gather | solution.py:36
  89.9 12.2 %all-to-all-start.1 = ((f32[16,1,2048]{2,1,0:T(1,128)}), f32[16,1,2048]{2,1,0:T(1,128)S(1)}, u32[]{:S(2)}, u32[]{:S(2)}) async-start(f32[16,1,2048]{2,1,0:T(1,128)} %reshape.248), calls=%async_computation.1 | async-start | bytes 262144 | tf_op jit(solution)/shard_map/all_to_all | solution.py:48
  113.2 22.9 %all-reduce.3 = (f32[64,64]{0,1:T(8,128)S(1)}, f32[64,64]{1,0:T(8,128)S(1)}, f32[64,64]{1,0:T(8,128)S(1)}) all-reduce(f32[64,64]{0,1:T(8,128)S(1)} %fusion.74, f32[64,64]{1,0:T(8,128)S(1)} %convolution_bitcast_fusion.6, f32[64,64]{1,0:T(8,128)S(1)} %fusion.54), channel_id=1, replica_groups=mesh['row_0'=8,'row_1'=4,'col_0'=8,'col_1'=2] {'row_0'}, use_global_device_ids=true, to_apply=%region_7.10 | all-reduce | flops 12288 | bytes 98304 | tf_op jit(solution)/shard_map/psum | solution.py:30
  136.1 14.2 %all-reduce.5 = (f32[64,64]{0,1:T(8,128)S(1)}, f32[64,64]{1,0:T(8,128)S(1)}, f32[64,64]{1,0:T(8,128)S(1)}) all-reduce(f32[64,64]{0,1:T(8,128)S(1)} %get-tuple-element.14, f32[64,64]{1,0:T(8,128)S(1)} %get-tuple-element.15, f32[64,64]{1,0:T(8,128)S(1)} %get-tuple-element.16), channel_id=1, replica_groups=mesh['row_0'=8,'row_1'=4,'col_0'=8,'col_1'=2] {'row_1'}, use_global_device_ids=true, to_apply=%region_8.11 | all-reduce | flops 12288 | bytes 98304 | tf_op jit(solution)/shard_map/psum | solution.py:30
  150.3 21.7 %all-reduce.1 = (f32[64,64]{0,1:T(8,128)S(1)}, f32[64,64]{1,0:T(8,128)S(1)}, f32[64,64]{1,0:T(8,128)S(1)}) all-reduce(f32[64,64]{0,1:T(8,128)S(1)} %get-tuple-element.20, f32[64,64]{1,0:T(8,128)S(1)} %get-tuple-element.21, f32[64,64]{1,0:T(8,128)S(1)} %get-tuple-element.22), channel_id=1, replica_groups=mesh['row_0'=8,'row_1'=4,'col_0'=8,'col_1'=2] {'col_0'}, use_global_device_ids=true, to_apply=%region_9.12 | all-reduce | flops 12288 | bytes 98304 | tf_op jit(solution)/shard_map/psum | solution.py:30
  172.0 21.3 %all-reduce.7 = (f32[64,64]{0,1:T(8,128)S(1)}, f32[64,64]{1,0:T(8,128)S(1)}, f32[64,64]{1,0:T(8,128)S(1)}) all-reduce(f32[64,64]{0,1:T(8,128)S(1)} %get-tuple-element.8, f32[64,64]{1,0:T(8,128)S(1)} %get-tuple-element.9, f32[64,64]{1,0:T(8,128)S(1)} %get-tuple-element.10), channel_id=1, replica_groups=mesh['row_0'=8,'row_1'=4,'col_0'=8,'col_1'=2] {'col_1'}, use_global_device_ids=true, to_apply=%region_10.13 | all-reduce | flops 12288 | bytes 98304 | tf_op jit(solution)/shard_map/psum | solution.py:30
  219.9 12.5 %all_to_all.31 = bf16[16,2,1024]{2,1,0:T(2,128)(2,1)S(1)} all-to-all(bf16[16,2,1024]{2,1,0:T(2,128)(2,1)S(1)} %reshape.250), channel_id=1, replica_groups=mesh['row_0'=8,'row_1'=4,'col_0'=8,'col_1'=2] {'col_0','col_1'}, dimensions={0} | all-to-all | bytes 131072 | tf_op jit(solution)/shard_map/all_to_all | solution.py:17
  232.7 10.1 %all_gather.20 = bf16[64,4,512]{2,0,1:T(8,128)(2,1)} all-gather(bf16[64,1,512]{2,0,1:T(8,128)(2,1)S(1)} %copy.97), channel_id=1, replica_groups=mesh['row_0'=8,'row_1'=4,'col_0'=8,'col_1'=2] {'row_1'}, dimensions={1}, use_global_device_ids=true | all-gather | bytes 327680 | tf_op jit(solution)/shard_map/all_gather | solution.py:36
  248.9 28.9 %all-gather.6.cloned.1.call-done = bf16[64,32,512]{2,0,1:T(8,128)(2,1)} async-done(((bf16[64,4,512]{2,0,1:T(8,128)(2,1)}), bf16[64,32,512]{2,0,1:T(8,128)(2,1)}) %all-gather.6.cloned.1.call-update) | async-done | bytes 2097168 | tf_op jit(solution)/shard_map/all_gather | solution.py:36
  291.4 12.2 %all-to-all-start.3 = ((f32[16,1,2048]{2,1,0:T(1,128)}), f32[16,1,2048]{2,1,0:T(1,128)S(1)}, u32[]{:S(2)}, u32[]{:S(2)}) async-start(f32[16,1,2048]{2,1,0:T(1,128)} %reshape.252), calls=%async_computation.3 | async-start | bytes 262144 | tf_op jit(solution)/shard_map/all_to_all | solution.py:48
  314.3 22.9 %all-reduce.2 = (f32[64,64]{1,0:T(8,128)S(1)}, f32[64,64]{1,0:T(8,128)S(1)}, f32[64,64]{1,0:T(8,128)S(1)}) all-reduce(f32[64,64]{1,0:T(8,128)S(1)} %fusion.78, f32[64,64]{1,0:T(8,128)S(1)} %fusion.81, f32[64,64]{1,0:T(8,128)S(1)} %fusion.79), channel_id=1, replica_groups=mesh['row_0'=8,'row_1'=4,'col_0'=8,'col_1'=2] {'row_0'}, use_global_device_ids=true, to_apply=%region_16.20 | all-reduce | flops 12288 | bytes 98304 | tf_op jit(solution)/shard_map/psum | solution.py:30
  337.2 14.2 %all-reduce.4 = (f32[64,64]{1,0:T(8,128)S(1)}, f32[64,64]{1,0:T(8,128)S(1)}, f32[64,64]{1,0:T(8,128)S(1)}) all-reduce(f32[64,64]{1,0:T(8,128)S(1)} %get-tuple-element.11, f32[64,64]{1,0:T(8,128)S(1)} %get-tuple-element.12, f32[64,64]{1,0:T(8,128)S(1)} %get-tuple-element.13), channel_id=1, replica_groups=mesh['row_0'=8,'row_1'=4,'col_0'=8,'col_1'=2] {'row_1'}, use_global_device_ids=true, to_apply=%region_17.21 | all-reduce | flops 12288 | bytes 98304 | tf_op jit(solution)/shard_map/psum | solution.py:30
  351.4 21.6 %all-reduce = (f32[64,64]{1,0:T(8,128)S(1)}, f32[64,64]{1,0:T(8,128)S(1)}, f32[64,64]{1,0:T(8,128)S(1)}) all-reduce(f32[64,64]{1,0:T(8,128)S(1)} %get-tuple-element.17, f32[64,64]{1,0:T(8,128)S(1)} %get-tuple-element.18, f32[64,64]{1,0:T(8,128)S(1)} %get-tuple-element.19), channel_id=1, replica_groups=mesh['row_0'=8,'row_1'=4,'col_0'=8,'col_1'=2] {'col_0'}, use_global_device_ids=true, to_apply=%region_18.22 | all-reduce | flops 12288 | bytes 98304 | tf_op jit(solution)/shard_map/psum | solution.py:30
  373.0 21.5 %all-reduce.6 = (f32[64,64]{1,0:T(8,128)S(1)}, f32[64,64]{1,0:T(8,128)S(1)}, f32[64,64]{1,0:T(8,128)S(1)}) all-reduce(f32[64,64]{1,0:T(8,128)S(1)} %get-tuple-element.4, f32[64,64]{1,0:T(8,128)S(1)} %get-tuple-element.6, f32[64,64]{1,0:T(8,128)S(1)} %get-tuple-element.7), channel_id=1, replica_groups=mesh['row_0'=8,'row_1'=4,'col_0'=8,'col_1'=2] {'col_1'}, use_global_device_ids=true, to_apply=%region_19.23 | all-reduce | flops 12288 | bytes 98304 | tf_op jit(solution)/shard_map/psum | solution.py:30
  408.9 12.3 %all_to_all.32 = bf16[16,2,1024]{2,1,0:T(2,128)(2,1)S(1)} all-to-all(bf16[16,2,1024]{2,1,0:T(2,128)(2,1)S(1)} %reshape.254), channel_id=1, replica_groups=mesh['row_0'=8,'row_1'=4,'col_0'=8,'col_1'=2] {'col_0','col_1'}, dimensions={0} | all-to-all | bytes 131072 | tf_op jit(solution)/shard_map/all_to_all | solution.py:17
  421.5 10.1 %all_gather.22 = bf16[64,4,512]{2,0,1:T(8,128)(2,1)} all-gather(bf16[64,1,512]{2,0,1:T(8,128)(2,1)S(1)} %copy.108), channel_id=1, replica_groups=mesh['row_0'=8,'row_1'=4,'col_0'=8,'col_1'=2] {'row_1'}, dimensions={1}, use_global_device_ids=true | all-gather | bytes 327680 | tf_op jit(solution)/shard_map/all_gather | solution.py:36
  431.6 34.9 %all-gather.8.cloned.1.call-done = bf16[64,32,512]{2,0,1:T(8,128)(2,1)} async-done(((bf16[64,4,512]{2,0,1:T(8,128)(2,1)}), bf16[64,32,512]{2,0,1:T(8,128)(2,1)}) %all-gather.8.cloned.1.call-update) | async-done | bytes 2097168 | tf_op jit(solution)/shard_map/all_gather | solution.py:36
  480.1 12.2 %all-to-all-start.5 = ((f32[16,1,2048]{2,1,0:T(1,128)}), f32[16,1,2048]{2,1,0:T(1,128)S(1)}, u32[]{:S(2)}, u32[]{:S(2)}) async-start(f32[16,1,2048]{2,1,0:T(1,128)} %reshape.256), calls=%async_computation.5 | async-start | bytes 262144 | tf_op jit(solution)/shard_map/all_to_all | solution.py:48
  502.6 22.1 %psum.232 = f32[64,64]{1,0:T(8,128)S(1)} all-reduce(f32[64,64]{1,0:T(8,128)S(1)} %fusion.53), channel_id=1, replica_groups=mesh['row_0'=8,'row_1'=4,'col_0'=8,'col_1'=2] {'row_0'}, use_global_device_ids=true, to_apply=%region_29.33 | all-reduce | flops 4096 | bytes 32768 | tf_op jit(solution)/shard_map/psum | solution.py:30
  524.6 13.2 %psum.233 = f32[64,64]{1,0:T(8,128)S(1)} all-reduce(f32[64,64]{1,0:T(8,128)S(1)} %psum.232), channel_id=1, replica_groups=mesh['row_0'=8,'row_1'=4,'col_0'=8,'col_1'=2] {'row_1'}, use_global_device_ids=true, to_apply=%region_30.34 | all-reduce | flops 4096 | bytes 32768 | tf_op jit(solution)/shard_map/psum | solution.py:30
  537.9 20.4 %psum.234 = f32[64,64]{1,0:T(8,128)S(1)} all-reduce(f32[64,64]{1,0:T(8,128)S(1)} %psum.233), channel_id=1, replica_groups=mesh['row_0'=8,'row_1'=4,'col_0'=8,'col_1'=2] {'col_0'}, use_global_device_ids=true, to_apply=%region_31.35 | all-reduce | flops 4096 | bytes 32768 | tf_op jit(solution)/shard_map/psum | solution.py:30
  558.2 21.0 %psum.235 = f32[64,64]{1,0:T(8,128)S(1)} all-reduce(f32[64,64]{1,0:T(8,128)S(1)} %psum.234), channel_id=1, replica_groups=mesh['row_0'=8,'row_1'=4,'col_0'=8,'col_1'=2] {'col_1'}, use_global_device_ids=true, to_apply=%region_32.36 | all-reduce | flops 4096 | bytes 32768 | tf_op jit(solution)/shard_map/psum | solution.py:30
  (146 shorter events, 136.7 us)
Async XLA Ops:
  7.2 78.8 %copy-start = (bf16[1,32,1,128,128]{4,3,2,1,0:T(8,128)(2,1)S(1)}, bf16[1,32,1,128,128]{4,3,2,1,0:T(8,128)(2,1)}, u32[]{:S(2)}) copy-start(bf16[1,32,1,128,128]{4,3,2,1,0:T(8,128)(2,1)} %param.13) | copy-start | bytes 3145732
  7.2 69.1 %all-gather.4.cloned.1.call-start = ((), (), s32[]{:S(2)}) async-start(), calls=%async_computation.6 | async-start | bytes 2359296 | tf_op jit(solution)/shard_map/all_gather | solution.py:36
  84.6 3.3 copy-start.3
  86.0 16.2 %copy-start.1 = (f32[64,32]{0,1:T(8,128)S(1)}, f32[64,32]{0,1:T(8,128)}, u32[]{:S(2)}) copy-start(f32[64,32]{0,1:T(8,128)} %param.11) | copy-start | bytes 24580
  87.9 24.7 %copy-start.2 = (f32[32]{0:T(128)S(1)}, f32[32]{0:T(128)}, u32[]{:S(2)}) copy-start(f32[32]{0:T(128)} %param.12) | copy-start | bytes 388
  89.9 21.1 %all-to-all-start.1 = ((f32[16,1,2048]{2,1,0:T(1,128)}), f32[16,1,2048]{2,1,0:T(1,128)S(1)}, u32[]{:S(2)}, u32[]{:S(2)}) async-start(f32[16,1,2048]{2,1,0:T(1,128)} %reshape.248), calls=%async_computation.1 | async-start | bytes 262144 | tf_op jit(solution)/shard_map/all_to_all | solution.py:48
  102.1 175.6 %all-gather.6.cloned.1.call-start = ((), (), s32[]{:S(2)}) async-start(), calls=%async_computation.7 | async-start | bytes 2359296 | tf_op jit(solution)/shard_map/all_gather | solution.py:36
  291.4 21.1 %all-to-all-start.3 = ((f32[16,1,2048]{2,1,0:T(1,128)}), f32[16,1,2048]{2,1,0:T(1,128)S(1)}, u32[]{:S(2)}, u32[]{:S(2)}) async-start(f32[16,1,2048]{2,1,0:T(1,128)} %reshape.252), calls=%async_computation.3 | async-start | bytes 262144 | tf_op jit(solution)/shard_map/all_to_all | solution.py:48
  303.5 163.0 %all-gather.8.cloned.1.call-start = ((), (), s32[]{:S(2)}) async-start(), calls=%async_computation.8 | async-start | bytes 2359296 | tf_op jit(solution)/shard_map/all_gather | solution.py:36
  480.1 21.1 %all-to-all-start.5 = ((f32[16,1,2048]{2,1,0:T(1,128)}), f32[16,1,2048]{2,1,0:T(1,128)S(1)}, u32[]{:S(2)}, u32[]{:S(2)}) async-start(f32[16,1,2048]{2,1,0:T(1,128)} %reshape.256), calls=%async_computation.5 | async-start | bytes 262144 | tf_op jit(solution)/shard_map/all_to_all | solution.py:48
Sparse Core Ops, SparseCore 0:
  38.4 37.8 all-gather.3
  243.0 34.7 all-gather.5
  431.7 34.7 all-gather.7
